TPU v7x, 32 devices: a whole 2x2x4 slice. The times are simulated.
32 devices in a mesh: dop: 2 (over y), rng: 16 (over z, x, core).
Axes of the slice: x: 2, y: 2, z: 4, core: 2. Of those that a mesh axis runs over, the one named last changes fastest.
Arguments:
- radar_cube: bfloat16 [2, 128, 1024, 512], P(None, 'dop', 'rng'), may hold values from -40 to 40
- train_gates: int32 [2, 768], P('dop', 'rng'), may hold values from 0 to 63, as said below
- look_angles: int32 [2, 8], P('dop'), may hold values from 0 to 255
Outputs:
- filtered: float32 [2, 2, 8, 1024], P(None, 'dop', None, 'rng')
Inputs may be any that keep to these rules, and one draw needn't show every extreme that they name: `train_gates`: entries k * 48 to (k + 1) * 48 - 1 of a bin's row list in increasing order the gates of the k-th block of 64 consecutive range gates, counted from that block's first gate, that lie outside one run of 16 consecutive gates of the block.
All inputs are finite; a program needn't handle non-finite values.
Results may differ from a plain program's by a relative error of at most 0.014.
The roundings to bfloat16 on the way count: a program that leaves them out, or rounds other values in their place, can miss the bound.
Values may be sent and summed in bfloat16 or wider, within the bound.
No kernel may reach another device: no remote copies, remote signals or barrier semaphores. Data moves between devices by JAX's collectives and lax.ppermute only.
A program may use at most 64 MiB of HBM per device.

v0:
```python
import math
import jax
import jax.numpy as jnp
from jax import lax
from jax.sharding import PartitionSpec as P

P_SIZE = 128
NANG = 256
load_eps = 1e-05


def doppler_table(bin_count, pulses):
    bin_freq = jnp.arange(bin_count, dtype=jnp.int32) * (pulses // bin_count)
    pulse_index = jnp.arange(pulses, dtype=jnp.int32)
    phase = (bin_freq[:, None] * pulse_index[None, :] % pulses).astype(jnp.float32) * (
        2.0 * math.pi / pulses
    )
    cosine = jnp.cos(phase).astype(jnp.bfloat16)
    sine = jnp.sin(phase).astype(jnp.bfloat16)
    upper = jnp.concatenate([cosine, sine], 1)
    lower = jnp.concatenate([-sine, cosine], 1)
    return jnp.concatenate([upper, lower], 0)


def gram_terms(train_rows):
    real_part = train_rows[0]
    imag_part = train_rows[1]
    contract = (((0,), (0,)), ((), ()))
    stacked = jnp.concatenate([real_part, imag_part], 0)
    power_sum = lax.dot_general(stacked, stacked, contract, preferred_element_type=jnp.float32)
    left_rows = jnp.concatenate([real_part, -imag_part], 0)
    right_rows = jnp.concatenate([imag_part, real_part], 0)
    cross_sum = lax.dot_general(left_rows, right_rows, contract, preferred_element_type=jnp.float32)
    return (power_sum, cross_sum)


def solve_weights(power_sum, cross_sum, look_row, train_count, angle_count):
    channels = power_sum.shape[0]
    top_half = jnp.concatenate([power_sum, cross_sum], 1)
    bottom_half = jnp.concatenate([cross_sum.T, power_sum], 1)
    covariance = jnp.concatenate([top_half, bottom_half], 0) / train_count
    loading = load_eps * jnp.trace(covariance) / (2 * channels)
    covariance = covariance + loading * jnp.eye(2 * channels, dtype=jnp.float32)
    factor = jnp.linalg.cholesky(covariance)
    channel_index = jnp.arange(channels, dtype=jnp.int32)
    slope = 2 * look_row + 1 - angle_count
    modulus = channel_index[:, None] * slope[None, :] % (2 * angle_count)
    phase = modulus.astype(jnp.float32) * (math.pi / angle_count)
    steering = jnp.concatenate([jnp.cos(phase), jnp.sin(phase)], 0)
    whitened = jax.scipy.linalg.solve_triangular(factor, steering, lower=True)
    lengths = jnp.sqrt(jnp.sum(whitened * whitened, axis=0))
    weights = jax.scipy.linalg.solve_triangular(
        factor, whitened / lengths[None, :], trans=1, lower=True
    )
    return weights.astype(jnp.bfloat16)


def filter_gates(spectrum, weights):
    direct = jnp.concatenate([spectrum[0], spectrum[1]], 1)
    rotated = jnp.concatenate([-spectrum[1], spectrum[0]], 1)
    contract = (((0,), (1,)), ((), ()))
    real_out = lax.dot_general(weights, direct, contract, preferred_element_type=jnp.float32)
    imag_out = lax.dot_general(weights, rotated, contract, preferred_element_type=jnp.float32)
    return jnp.stack([real_out, imag_out])


def pack_terms(power_part, cross_part, lower_mask):
    return jnp.where(lower_mask, power_part, cross_part)


def unpack_terms(packed, row_index, col_index):
    lower_mask = row_index >= col_index
    lower_part = jnp.where(lower_mask, packed, 0.0)
    strict_lower = jnp.where(row_index > col_index, packed, 0.0)
    power_sum = lower_part + strict_lower.T
    upper_part = jnp.where(lower_mask, 0.0, packed)
    cross_sum = upper_part - upper_part.T
    return (power_sum, cross_sum)


def on_device(radar_cube, train_gates, look_angles):
    dop_count = lax.axis_size("dop")
    rng_count = lax.axis_size("rng")
    bin_local = train_gates.shape[0]
    bin_count = dop_count * bin_local
    dft_table = doppler_table(bin_count, P_SIZE)
    norm_scale = 1.0 / math.sqrt(P_SIZE)
    segment = lax.all_to_all(radar_cube, "dop", split_axis=2, concat_axis=1, tiled=True)
    flattened = segment.reshape(2 * P_SIZE, -1)
    spectral = (
        jnp.dot(dft_table, flattened, preferred_element_type=jnp.float32) * norm_scale
    ).astype(jnp.bfloat16)
    spectral = spectral.reshape(2, bin_count, segment.shape[2], segment.shape[3])
    binned = lax.all_to_all(spectral, "dop", split_axis=1, concat_axis=2, tiled=True)
    channels = binned.shape[3]
    train_count = train_gates.shape[1] * rng_count
    row_index = lax.broadcasted_iota(jnp.int32, (channels, channels), 0)
    col_index = lax.broadcasted_iota(jnp.int32, (channels, channels), 1)
    lower_mask = row_index >= col_index
    rows = jnp.take(binned[:, 0], train_gates[0], axis=1)
    power_part, cross_part = gram_terms(rows)
    packed_all = jnp.stack([pack_terms(power_part, cross_part, lower_mask)])
    summed = lax.psum(packed_all, "rng")

    def unpack_one(packed):
        return unpack_terms(packed, row_index, col_index)

    power_all, cross_all = jax.vmap(unpack_one)(summed)

    def solve_one(inputs):
        return solve_weights(inputs[0], inputs[1], inputs[2], train_count, NANG)

    weights_all = lax.map(solve_one, (power_all, cross_all, look_angles))
    outputs = [filter_gates(binned[:, 0], weights_all[0])]
    return jnp.stack(outputs, 1)


def solution(mesh):
    placed = (P(None, "dop", "rng", None), P("dop", "rng"), P("dop", None))
    return jax.shard_map(
        on_device,
        mesh=mesh,
        in_specs=placed,
        out_specs=P(None, "dop", None, "rng"),
        check_vma=False,
    )
```

profile of v0, /device:TPU:0, one launch (start us, length us, event | category | flops | bytes accessed | tf_op | source)
XLA Modules:
  0.0 629.6 jit_solution(5859860382280964349)
XLA Ops:
  6.5 11.3 %copy.107 = bf16[2,64,64,512]{3,1,0,2:T(8,128)(2,1)} copy(bf16[2,64,64,512]{3,2,1,0:T(8,128)(2,1)} %param.3) | data formatting | bytes 16777216 | tf_op args[0]
  17.9 7.2 %all-to-all-start = ((bf16[2,64,64,512]{3,1,0,2:T(8,128)(2,1)}), bf16[2,64,64,512]{3,1,0,2:T(8,128)(2,1)}, u32[]{:S(2)}, u32[]{:S(2)}) async-start(bf16[2,64,64,512]{3,1,0,2:T(8,128)(2,1)} %copy.107), calls=%async_computation | async-start | bytes 16777216 | tf_op jit(solution)/shard_map/all_to_all | solution.py:88
  26.1 92.9 %all-to-all-done = bf16[2,64,64,512]{3,1,0,2:T(8,128)(2,1)} async-done(((bf16[2,64,64,512]{3,1,0,2:T(8,128)(2,1)}), bf16[2,64,64,512]{3,1,0,2:T(8,128)(2,1)}, u32[]{:S(2)}, u32[]{:S(2)}) %all-to-all-start) | async-done | bytes 8388640 | tf_op jit(solution)/shard_map/all_to_all | solution.py:88
  119.0 11.4 %copy.108 = bf16[2,64,2,32,512]{4,3,1,2,0:T(8,128)(2,1)} copy(bf16[2,64,2,32,512]{4,1,0,3,2:T(8,128)(2,1)} %bitcast.1) | data formatting | bytes 16777216 | tf_op jit(solution)/shard_map/all_to_all | solution.py:88
  130.4 15.6 %copy.155 = bf16[32,8,32,512]{3,1,2,0:T(8,128)(2,1)} copy(bf16[32,8,32,512]{3,2,1,0:T(8,128)(2,1)} %bitcast.183) | data formatting | bytes 16777216
  146.0 4.6 fusion
  151.3 3.4 all-to-all-start.1
  154.7 4.4 all-to-all-done.1
  160.7 1.3 fusion.2
  162.1 94.4 %all-reduce.3.cloned.1.call-done = f32[1,512,512]{2,1,0:T(8,128)} async-done(((f32[1,512,512]{2,1,0:T(8,128)}), f32[1,512,512]{2,1,0:T(8,128)}) %all-reduce.3.cloned.1.call-update) | async-done | bytes 1048592 | tf_op jit(solution)/shard_map/psum | solution.py:103
  256.5 1.5 broadcast_select_fusion
  258.0 1.3 copy.115
  259.3 1.4 copy.111
  260.7 3.3 fusion.11
  264.0 1.6 copy.116
  267.1 2.6 select_add_fusion
  269.7 5.7 copy.117
  275.4 3.2 fusion.1
  278.6 1.9 copy-done.1
  280.6 11.7 %cholesky.222 = f32[128,128]{1,0:T(8,128)S(1)} custom-call(f32[128,128]{1,0:T(8,128)S(1)} %cholesky.577), custom_call_target="Cholesky" | custom-call | tf_op jit(solution)/shard_map/while/body/eval_jaxpr/jit(cholesky)/cholesky | solution.py:44
  292.3 9.8 %custom-call.82 = f32[1,128,128]{1,2,0:T(8,128)S(1)} custom-call(f32[1,128,128]{2,1,0:T(8,128)S(1)} %get-tuple-element.79), custom_call_target="InvertDiagBlocksLowerTriangular" | custom-call | tf_op jit(solution)/shard_map/while/body/eval_jaxpr/jit(cholesky)/cholesky | solution.py:44
  302.1 1.5 fusion.15
  303.7 1.6 convolution_subtract_fusion
  305.3 11.7 %cholesky.243 = f32[128,128]{1,0:T(8,128)S(1)} custom-call(f32[128,128]{1,0:T(8,128)S(1)} %cholesky.581), custom_call_target="Cholesky" | custom-call | tf_op jit(solution)/shard_map/while/body/eval_jaxpr/jit(cholesky)/cholesky | solution.py:44
  317.6 9.8 %custom-call.83 = f32[1,128,128]{1,2,0:T(8,128)S(1)} custom-call(f32[1,128,128]{2,1,0:T(8,128)S(1)} %get-tuple-element.77), custom_call_target="InvertDiagBlocksLowerTriangular" | custom-call | tf_op jit(solution)/shard_map/while/body/eval_jaxpr/jit(cholesky)/cholesky | solution.py:44
  328.5 2.0 copy-done
  330.5 2.4 convolution_subtract_fusion.1
  332.9 11.7 %cholesky.466 = f32[128,128]{1,0:T(8,128)S(1)} custom-call(f32[128,128]{1,0:T(8,128)S(1)} %cholesky.586), custom_call_target="Cholesky" | custom-call | tf_op jit(solution)/shard_map/while/body/eval_jaxpr/jit(cholesky)/cholesky | solution.py:44
  345.4 9.8 %custom-call.84 = f32[1,128,128]{1,2,0:T(8,128)S(1)} custom-call(f32[1,128,128]{2,1,0:T(8,128)S(1)} %get-tuple-element.75), custom_call_target="InvertDiagBlocksLowerTriangular" | custom-call | tf_op jit(solution)/shard_map/while/body/eval_jaxpr/jit(cholesky)/cholesky | solution.py:44
  355.2 1.3 convolution_dynamic-update-slice_fusion.1
  356.5 3.3 convolution_subtract_fusion.2
  359.8 11.7 %cholesky.485 = f32[128,128]{1,0:T(8,128)S(1)} custom-call(f32[128,128]{1,0:T(8,128)S(1)} %cholesky.591), custom_call_target="Cholesky" | custom-call | tf_op jit(solution)/shard_map/while/body/eval_jaxpr/jit(cholesky)/cholesky | solution.py:44
  372.3 9.8 %custom-call.85 = f32[1,128,128]{1,2,0:T(8,128)S(1)} custom-call(f32[1,128,128]{2,1,0:T(8,128)S(1)} %get-tuple-element.73), custom_call_target="InvertDiagBlocksLowerTriangular" | custom-call | tf_op jit(solution)/shard_map/while/body/eval_jaxpr/jit(cholesky)/cholesky | solution.py:44
  383.2 3.1 convolution_subtract_fusion.3
  386.4 12.1 %cholesky.504 = f32[128,128]{1,0:T(8,128)S(1)} custom-call(f32[128,128]{1,0:T(8,128)S(1)} %cholesky.596), custom_call_target="Cholesky" | custom-call | tf_op jit(solution)/shard_map/while/body/eval_jaxpr/jit(cholesky)/cholesky | solution.py:44
  399.3 9.8 %custom-call.86 = f32[1,128,128]{1,2,0:T(8,128)S(1)} custom-call(f32[1,128,128]{2,1,0:T(8,128)S(1)} %get-tuple-element.71), custom_call_target="InvertDiagBlocksLowerTriangular" | custom-call | tf_op jit(solution)/shard_map/while/body/eval_jaxpr/jit(cholesky)/cholesky | solution.py:44
  410.2 3.1 convolution_subtract_fusion.4
  413.3 11.7 %cholesky.524 = f32[128,128]{1,0:T(8,128)S(1)} custom-call(f32[128,128]{1,0:T(8,128)S(1)} %cholesky.601), custom_call_target="Cholesky" | custom-call | tf_op jit(solution)/shard_map/while/body/eval_jaxpr/jit(cholesky)/cholesky | solution.py:44
  425.8 9.8 %custom-call.87 = f32[1,128,128]{1,2,0:T(8,128)S(1)} custom-call(f32[1,128,128]{2,1,0:T(8,128)S(1)} %get-tuple-element.69), custom_call_target="InvertDiagBlocksLowerTriangular" | custom-call | tf_op jit(solution)/shard_map/while/body/eval_jaxpr/jit(cholesky)/cholesky | solution.py:44
  436.6 2.8 convolution_subtract_fusion.5
  439.4 11.7 %cholesky.544 = f32[128,128]{1,0:T(8,128)S(1)} custom-call(f32[128,128]{1,0:T(8,128)S(1)} %cholesky.606), custom_call_target="Cholesky" | custom-call | tf_op jit(solution)/shard_map/while/body/eval_jaxpr/jit(cholesky)/cholesky | solution.py:44
  451.9 9.8 %custom-call.88 = f32[1,128,128]{1,2,0:T(8,128)S(1)} custom-call(f32[1,128,128]{2,1,0:T(8,128)S(1)} %get-tuple-element.67), custom_call_target="InvertDiagBlocksLowerTriangular" | custom-call | tf_op jit(solution)/shard_map/while/body/eval_jaxpr/jit(cholesky)/cholesky | solution.py:44
  462.7 2.1 convolution_subtract_fusion.6
  464.8 11.7 %cholesky.562 = f32[128,128]{1,0:T(8,128)S(1)} custom-call(f32[128,128]{1,0:T(8,128)S(1)} %convolution_subtract_fusion.6), custom_call_target="Cholesky" | custom-call | tf_op jit(solution)/shard_map/while/body/eval_jaxpr/jit(cholesky)/cholesky | solution.py:44
  487.6 4.8 select_select_fusion
  492.4 28.5 %while.1 = (s32[]{:T(128)}, f32[1024,1024]{0,1:T(8,128)}, s32[8,2]{0,1:T(2,128)S(1)}, f32[8,128,128]{2,1,0:T(8,128)}, s32[]{:T(128)}) while((s32[]{:T(128)}, f32[1024,1024]{0,1:T(8,128)}, s32[8,2]{0,1:T(2,128)S(1)}, f32[8,128,128]{2,1,0:T(8,128)}, s32[]{:T(128)}) %tuple.66), condition=%wide.while_cond, body=%wide.while_body.sunk | while | flops 2 | bytes 393829 | solution.py:52
  493.0 2.2 dynamic-slice.7
  496.6 2.2 dynamic-slice.7
  500.2 2.2 dynamic-slice.7
  503.8 2.2 dynamic-slice.7
  507.3 2.2 dynamic-slice.7
  510.9 2.2 dynamic-slice.7
  514.5 2.2 dynamic-slice.7
  518.0 2.2 dynamic-slice.7
  520.9 79.6 %custom-call.89 = f32[8,128,128]{1,2,0:T(8,128)S(1)} custom-call(f32[8,128,128]{2,1,0:T(8,128)} %get-tuple-element.27), custom_call_target="InvertDiagBlocksLowerTriangular" | custom-call | tf_op jit(solution)/shard_map/while/body/eval_jaxpr/jit(_solve_triangular)/triangular_solve | solution.py:52
  604.5 1.2 convolution_subtract_fusion.13
  605.9 1.3 convolution_subtract_fusion.12
  607.3 1.3 convolution_subtract_fusion.20
  608.8 1.4 convolution_subtract_fusion.19
  613.4 1.2 convolution_subtract_fusion.9
  614.9 1.3 convolution_subtract_fusion.8
  616.5 1.4 convolution_subtract_fusion.7
  618.1 1.4 convolution_subtract_fusion.18
  619.8 1.5 convolution_subtract_fusion.17
  (164 shorter events, 40.5 us)
Async XLA Ops:
  17.9 7.7 %copy-start.4 = (s32[1,48]{1,0:T(1,128)S(1)}, s32[1,48]{1,0:T(1,128)}, u32[]{:S(2)}) copy-start(s32[1,48]{1,0:T(1,128)} %param.4) | copy-start | bytes 580
  17.9 7.9 %copy-start.5 = (s32[1,8]{1,0:T(1,128)S(1)}, s32[1,8]{1,0:T(1,128)}, u32[]{:S(2)}) copy-start(s32[1,8]{1,0:T(1,128)} %param.5) | copy-start | bytes 100
  17.9 101.1 %all-to-all-start = ((bf16[2,64,64,512]{3,1,0,2:T(8,128)(2,1)}), bf16[2,64,64,512]{3,1,0,2:T(8,128)(2,1)}, u32[]{:S(2)}, u32[]{:S(2)}) async-start(bf16[2,64,64,512]{3,1,0,2:T(8,128)(2,1)} %copy.107), calls=%async_computation | async-start | bytes 16777216 | tf_op jit(solution)/shard_map/all_to_all | solution.py:88
  151.3 7.8 %all-to-all-start.1 = ((bf16[2,2,32,512]{3,2,0,1:T(8,128)(2,1)}), bf16[2,2,32,512]{3,2,0,1:T(8,128)(2,1)S(1)}, u32[]{:S(2)}, u32[]{:S(2)}) async-start(bf16[2,2,32,512]{3,2,0,1:T(8,128)(2,1)} %copy.109), calls=%async_computation.1 | async-start | bytes 262144 | tf_op jit(solution)/shard_map/all_to_all | solution.py:94
  154.6 101.8 %all-reduce.3.cloned.1.call-start = ((), (), s32[]{:S(2)}) async-start(), calls=%async_computation.2 | async-start | bytes 2097152 | tf_op jit(solution)/shard_map/psum | solution.py:103
  256.5 2.8 copy-start.2
  257.9 1.3 copy-start.3
  278.6 1.9 copy-start.1
  328.5 2.0 copy-start
Sparse Core Ops, SparseCore 0:
  162.2 94.2 all-reduce.2
where the time goes:
time: 636 us; the launch traced here: 630 us
  other arithmetic  266 us (42%)
  waiting for transfers between devices  192 us (30%)
  local copies, waits for them, and re-layouts  88.4 us (14%)
  matrix products  52.9 us (8%)
  between operations  19.9 us (3%)
  starting transfers between devices  10.6 us (2%)
    another operation x31, other arithmetic, solve_weights(): factor = jnp.linalg.cholesky(covariance)  168 us
    psum x1, waiting for transfers between devices, on_device(): summed = lax.psum(packed_all, 'rng')  94.4 us
    all_to_all x1, waiting for transfers between devices, on_device(): lax.all_to_all(radar_cube, 'dop', split_axis=2, concat_axis=1, tiled=True)  92.9 us
    another operation x4, other arithmetic, solve_weights(): jax.scipy.linalg.solve_triangular(factor, whitened / lengths[None, :], tr...  84.4 us
    unnamed x29, local copies, waits for them, and re-layouts  31 us
    another operation x40, local copies, waits for them, and re-layouts  28.4 us
    another operation x14, matrix products, solve_weights(): factor = jnp.linalg.cholesky(covariance)  25.9 us
  transfers between devices with their start and end apart: 3, of which 3 were waited for; matrix products, arithmetic and copies ran while one was open for 0% of the time, Pallas kernels for 0%

commit v1 on v0

--- a/solution.py
+++ b/solution.py
@@ -1,3 +1,4 @@
+import functools
 import math
 import jax
 import jax.numpy as jnp
@@ -7,6 +8,13 @@
 P_SIZE = 128
 NANG = 256
 load_eps = 1e-05
+
+
+def reach_the_cube(q_in, along_axis):
+    return jnp.sum(lax.all_gather(q_in, along_axis), axis=0)
+
+
+serve_things = functools.partial(reach_the_cube, along_axis="rng")
 
 
 def doppler_table(bin_count, pulses):
@@ -100,7 +108,7 @@
     rows = jnp.take(binned[:, 0], train_gates[0], axis=1)
     power_part, cross_part = gram_terms(rows)
     packed_all = jnp.stack([pack_terms(power_part, cross_part, lower_mask)])
-    summed = lax.psum(packed_all, "rng")
+    summed = serve_things(packed_all)
 
     def unpack_one(packed):
         return unpack_terms(packed, row_index, col_index)

time: 636 us -> 677 us (1.064)
  waiting for transfers between devices: 192 us -> 224 us
    all_gather x0 -> x1, waiting for transfers between devices: none -> 126 us  [reach_the_cube(): return jnp.sum(lax.all_gather(q_in, along_axis), axis=0)]
    psum x1 -> x0, waiting for transfers between devices: 94.4 us -> none  [on_device(): summed = lax.psum(packed_all, 'rng')]
    reduce_sum x0 -> x1, other arithmetic: none -> 7.91 us  [reach_the_cube(): return jnp.sum(lax.all_gather(q_in, along_axis), axis=0)]
    unnamed x29 -> x25, local copies, waits for them, and re-layouts: 31 us -> 29 us
where the time goes in v1:
time: 677 us; the launch traced here: 671 us
  other arithmetic  272 us (40%)
  waiting for transfers between devices  224 us (33%)
  local copies, waits for them, and re-layouts  89.8 us (13%)
  matrix products  54 us (8%)
  between operations  19.9 us (3%)
  starting transfers between devices  10.6 us (2%)
    another operation x31, other arithmetic, solve_weights(): factor = jnp.linalg.cholesky(covariance)  168 us
    all_gather x1, waiting for transfers between devices, reach_the_cube(): return jnp.sum(lax.all_gather(q_in, along_axis), axis=0)  126 us
    all_to_all x1, waiting for transfers between devices, on_device(): lax.all_to_all(radar_cube, 'dop', split_axis=2, concat_axis=1, tiled=True)  93.6 us
    another operation x4, other arithmetic, solve_weights(): jax.scipy.linalg.solve_triangular(factor, whitened / lengths[None, :], tr...  84.4 us
    unnamed x25, local copies, waits for them, and re-layouts  29 us
    another operation x40, local copies, waits for them, and re-layouts  28.4 us
    another operation x14, matrix products, solve_weights(): factor = jnp.linalg.cholesky(covariance)  27 us
  transfers between devices with their start and end apart: 3, of which 3 were waited for; matrix products, arithmetic and copies ran while one was open for 0% of the time, Pallas kernels for 0%

profile of v1, /device:TPU:0, one launch (start us, length us, event | category | flops | bytes accessed | tf_op | source)
XLA Modules:
  0.0 671.3 jit_solution(929261290024821387)
XLA Ops:
  6.5 11.3 %copy.107 = bf16[2,64,64,512]{3,1,0,2:T(8,128)(2,1)} copy(bf16[2,64,64,512]{3,2,1,0:T(8,128)(2,1)} %param.3) | data formatting | bytes 16777216 | tf_op args[0]
  17.9 7.2 %all-to-all-start = ((bf16[2,64,64,512]{3,1,0,2:T(8,128)(2,1)}), bf16[2,64,64,512]{3,1,0,2:T(8,128)(2,1)}, u32[]{:S(2)}, u32[]{:S(2)}) async-start(bf16[2,64,64,512]{3,1,0,2:T(8,128)(2,1)} %copy.107), calls=%async_computation | async-start | bytes 16777216 | tf_op jit(solution)/shard_map/all_to_all | solution.py:96
  25.4 93.6 %all-to-all-done = bf16[2,64,64,512]{3,1,0,2:T(8,128)(2,1)} async-done(((bf16[2,64,64,512]{3,1,0,2:T(8,128)(2,1)}), bf16[2,64,64,512]{3,1,0,2:T(8,128)(2,1)}, u32[]{:S(2)}, u32[]{:S(2)}) %all-to-all-start) | async-done | bytes 8388640 | tf_op jit(solution)/shard_map/all_to_all | solution.py:96
  119.0 11.4 %copy.108 = bf16[2,64,2,32,512]{4,3,1,2,0:T(8,128)(2,1)} copy(bf16[2,64,2,32,512]{4,1,0,3,2:T(8,128)(2,1)} %bitcast.1) | data formatting | bytes 16777216 | tf_op jit(solution)/shard_map/all_to_all | solution.py:96
  130.4 15.6 %copy.156 = bf16[32,8,32,512]{3,1,2,0:T(8,128)(2,1)} copy(bf16[32,8,32,512]{3,2,1,0:T(8,128)(2,1)} %bitcast.185) | data formatting | bytes 16777216
  146.0 4.6 fusion
  151.3 3.4 all-to-all-start.1
  154.7 4.4 all-to-all-done.1
  160.7 1.3 convolution_select_fusion
  162.8 126.3 %all-gather.3.cloned.1.call-done = f32[8192,512]{1,0:T(8,128)} async-done(((f32[512,512]{1,0:T(8,128)}), f32[8192,512]{1,0:T(8,128)}) %all-gather.3.cloned.1.call-update) | async-done | bytes 16777232 | tf_op jit(solution)/shard_map/all_gather | solution.py:14
  289.1 7.9 %reduce.65 = f32[512,512]{1,0:T(8,128)S(1)} reduce(f32[16,512,512]{2,1,0:T(8,128)} %bitcast.186, f32[]{:T(128)} %constant.370.clone.1), dimensions={0}, to_apply=%region_0.1 | reduce | flops 3932160 | bytes 17825796 | tf_op jit(solution)/shard_map/reduce_sum | solution.py:14
  297.2 1.3 copy.115
  298.5 1.4 copy.111
  299.9 3.3 fusion.10
  303.2 1.6 copy.116
  306.3 2.6 select_add_fusion
  308.9 5.7 copy.117
  314.6 3.2 fusion.1
  317.8 1.9 copy-done
  319.8 11.7 %cholesky.222 = f32[128,128]{1,0:T(8,128)S(1)} custom-call(f32[128,128]{1,0:T(8,128)S(1)} %cholesky.577), custom_call_target="Cholesky" | custom-call | tf_op jit(solution)/shard_map/while/body/eval_jaxpr/jit(cholesky)/cholesky | solution.py:52
  331.5 9.8 %custom-call.82 = f32[1,128,128]{1,2,0:T(8,128)S(1)} custom-call(f32[1,128,128]{2,1,0:T(8,128)S(1)} %get-tuple-element.79), custom_call_target="InvertDiagBlocksLowerTriangular" | custom-call | tf_op jit(solution)/shard_map/while/body/eval_jaxpr/jit(cholesky)/cholesky | solution.py:52
  341.3 1.5 fusion.14
  342.9 1.6 convolution_subtract_fusion
  344.5 11.7 %cholesky.243 = f32[128,128]{1,0:T(8,128)S(1)} custom-call(f32[128,128]{1,0:T(8,128)S(1)} %cholesky.581), custom_call_target="Cholesky" | custom-call | tf_op jit(solution)/shard_map/while/body/eval_jaxpr/jit(cholesky)/cholesky | solution.py:52
  356.8 2.5 cholesky.254
  359.3 9.8 %custom-call.83 = f32[1,128,128]{1,2,0:T(8,128)S(1)} custom-call(f32[1,128,128]{2,1,0:T(8,128)S(1)} %get-tuple-element.77), custom_call_target="InvertDiagBlocksLowerTriangular" | custom-call | tf_op jit(solution)/shard_map/while/body/eval_jaxpr/jit(cholesky)/cholesky | solution.py:52
  370.5 1.3 convolution_dynamic-update-slice_fusion
  371.9 2.7 convolution_subtract_fusion.1
  374.6 11.7 %cholesky.466 = f32[128,128]{1,0:T(8,128)S(1)} custom-call(f32[128,128]{1,0:T(8,128)S(1)} %cholesky.586), custom_call_target="Cholesky" | custom-call | tf_op jit(solution)/shard_map/while/body/eval_jaxpr/jit(cholesky)/cholesky | solution.py:52
  387.1 9.8 %custom-call.84 = f32[1,128,128]{1,2,0:T(8,128)S(1)} custom-call(f32[1,128,128]{2,1,0:T(8,128)S(1)} %get-tuple-element.75), custom_call_target="InvertDiagBlocksLowerTriangular" | custom-call | tf_op jit(solution)/shard_map/while/body/eval_jaxpr/jit(cholesky)/cholesky | solution.py:52
  396.9 1.3 convolution_dynamic-update-slice_fusion.1
  398.1 3.3 convolution_subtract_fusion.2
  401.5 11.7 %cholesky.485 = f32[128,128]{1,0:T(8,128)S(1)} custom-call(f32[128,128]{1,0:T(8,128)S(1)} %cholesky.591), custom_call_target="Cholesky" | custom-call | tf_op jit(solution)/shard_map/while/body/eval_jaxpr/jit(cholesky)/cholesky | solution.py:52
  414.0 9.8 %custom-call.85 = f32[1,128,128]{1,2,0:T(8,128)S(1)} custom-call(f32[1,128,128]{2,1,0:T(8,128)S(1)} %get-tuple-element.73), custom_call_target="InvertDiagBlocksLowerTriangular" | custom-call | tf_op jit(solution)/shard_map/while/body/eval_jaxpr/jit(cholesky)/cholesky | solution.py:52
  424.9 3.1 convolution_subtract_fusion.3
  428.1 12.1 %cholesky.504 = f32[128,128]{1,0:T(8,128)S(1)} custom-call(f32[128,128]{1,0:T(8,128)S(1)} %cholesky.596), custom_call_target="Cholesky" | custom-call | tf_op jit(solution)/shard_map/while/body/eval_jaxpr/jit(cholesky)/cholesky | solution.py:52
  440.9 9.8 %custom-call.86 = f32[1,128,128]{1,2,0:T(8,128)S(1)} custom-call(f32[1,128,128]{2,1,0:T(8,128)S(1)} %get-tuple-element.71), custom_call_target="InvertDiagBlocksLowerTriangular" | custom-call | tf_op jit(solution)/shard_map/while/body/eval_jaxpr/jit(cholesky)/cholesky | solution.py:52
  451.9 3.1 convolution_subtract_fusion.4
  455.0 11.7 %cholesky.524 = f32[128,128]{1,0:T(8,128)S(1)} custom-call(f32[128,128]{1,0:T(8,128)S(1)} %cholesky.601), custom_call_target="Cholesky" | custom-call | tf_op jit(solution)/shard_map/while/body/eval_jaxpr/jit(cholesky)/cholesky | solution.py:52
  467.4 9.8 %custom-call.87 = f32[1,128,128]{1,2,0:T(8,128)S(1)} custom-call(f32[1,128,128]{2,1,0:T(8,128)S(1)} %get-tuple-element.69), custom_call_target="InvertDiagBlocksLowerTriangular" | custom-call | tf_op jit(solution)/shard_map/while/body/eval_jaxpr/jit(cholesky)/cholesky | solution.py:52
  478.2 2.8 convolution_subtract_fusion.5
  481.1 11.7 %cholesky.544 = f32[128,128]{1,0:T(8,128)S(1)} custom-call(f32[128,128]{1,0:T(8,128)S(1)} %cholesky.606), custom_call_target="Cholesky" | custom-call | tf_op jit(solution)/shard_map/while/body/eval_jaxpr/jit(cholesky)/cholesky | solution.py:52
  493.6 9.8 %custom-call.88 = f32[1,128,128]{1,2,0:T(8,128)S(1)} custom-call(f32[1,128,128]{2,1,0:T(8,128)S(1)} %get-tuple-element.67), custom_call_target="InvertDiagBlocksLowerTriangular" | custom-call | tf_op jit(solution)/shard_map/while/body/eval_jaxpr/jit(cholesky)/cholesky | solution.py:52
  504.3 2.1 convolution_subtract_fusion.6
  506.4 11.7 %cholesky.562 = f32[128,128]{1,0:T(8,128)S(1)} custom-call(f32[128,128]{1,0:T(8,128)S(1)} %convolution_subtract_fusion.6), custom_call_target="Cholesky" | custom-call | tf_op jit(solution)/shard_map/while/body/eval_jaxpr/jit(cholesky)/cholesky | solution.py:52
  529.2 4.8 select_select_fusion
  534.1 28.5 %while.1 = (s32[]{:T(128)}, f32[1024,1024]{0,1:T(8,128)}, s32[8,2]{0,1:T(2,128)S(1)}, f32[8,128,128]{2,1,0:T(8,128)}, s32[]{:T(128)}) while((s32[]{:T(128)}, f32[1024,1024]{0,1:T(8,128)}, s32[8,2]{0,1:T(2,128)S(1)}, f32[8,128,128]{2,1,0:T(8,128)}, s32[]{:T(128)}) %tuple.66), condition=%wide.while_cond, body=%wide.while_body.sunk | while | flops 2 | bytes 393829 | solution.py:60
  534.7 2.2 dynamic-slice.7
  538.3 2.2 dynamic-slice.7
  541.8 2.2 dynamic-slice.7
  545.4 2.2 dynamic-slice.7
  549.0 2.2 dynamic-slice.7
  552.5 2.2 dynamic-slice.7
  556.1 2.2 dynamic-slice.7
  559.7 2.2 dynamic-slice.7
  562.6 79.6 %custom-call.89 = f32[8,128,128]{1,2,0:T(8,128)S(1)} custom-call(f32[8,128,128]{2,1,0:T(8,128)} %get-tuple-element.27), custom_call_target="InvertDiagBlocksLowerTriangular" | custom-call | tf_op jit(solution)/shard_map/while/body/eval_jaxpr/jit(_solve_triangular)/triangular_solve | solution.py:60
  647.5 1.3 convolution_subtract_fusion.12
  648.9 1.3 convolution_subtract_fusion.20
  650.4 1.4 convolution_subtract_fusion.19
  655.1 1.2 convolution_subtract_fusion.9
  656.5 1.3 convolution_subtract_fusion.8
  658.1 1.4 convolution_subtract_fusion.7
  659.8 1.4 convolution_subtract_fusion.18
  661.4 1.5 convolution_subtract_fusion.17
  (161 shorter events, 42.2 us)
Async XLA Ops:
  17.9 7.2 %copy-start.2 = (s32[1,48]{1,0:T(1,128)S(1)}, s32[1,48]{1,0:T(1,128)}, u32[]{:S(2)}) copy-start(s32[1,48]{1,0:T(1,128)} %param.4) | copy-start | bytes 580
  17.9 101.1 %all-to-all-start = ((bf16[2,64,64,512]{3,1,0,2:T(8,128)(2,1)}), bf16[2,64,64,512]{3,1,0,2:T(8,128)(2,1)}, u32[]{:S(2)}, u32[]{:S(2)}) async-start(bf16[2,64,64,512]{3,1,0,2:T(8,128)(2,1)} %copy.107), calls=%async_computation | async-start | bytes 16777216 | tf_op jit(solution)/shard_map/all_to_all | solution.py:96
  150.6 12.0 %copy-start.3 = (s32[1,8]{1,0:T(1,128)S(1)}, s32[1,8]{1,0:T(1,128)}, u32[]{:S(2)}) copy-start(s32[1,8]{1,0:T(1,128)} %param.5) | copy-start | bytes 100
  151.3 7.8 %all-to-all-start.1 = ((bf16[2,2,32,512]{3,2,0,1:T(8,128)(2,1)}), bf16[2,2,32,512]{3,2,0,1:T(8,128)(2,1)S(1)}, u32[]{:S(2)}, u32[]{:S(2)}) async-start(bf16[2,2,32,512]{3,2,0,1:T(8,128)(2,1)} %copy.109), calls=%async_computation.1 | async-start | bytes 262144 | tf_op jit(solution)/shard_map/all_to_all | solution.py:102
  154.6 134.4 %all-gather.3.cloned.1.call-start = ((), (), s32[]{:S(2)}) async-start(), calls=%async_computation.2 | async-start | bytes 17825792 | tf_op jit(solution)/shard_map/all_gather | solution.py:14
  297.1 1.3 copy-start.1
  317.8 1.9 copy-start
Sparse Core Ops, SparseCore 0:
  162.2 126.8 all-gather.2
